TPU v7x, 512 devices: a whole 4x8x8 slice. The times are simulated.
512 devices in a mesh: fibre: 16 (over y, core), col: 32 (over x, z).
Axes of the slice: x: 4, y: 8, z: 8, core: 2. Of those that a mesh axis runs over, the one named last changes fastest.
Arguments:
- field: float32 [640, 160, 4096], P('fibre', None, 'col'), may hold values from -180 to 180, as said below
- start: float32 [640, 160], replicated, may hold values from -6 to 6
Outputs:
- basis: float32 [640, 160], replicated
- core: float32 [160, 160, 4096], P(None, 'fibre', 'col')
Inputs may be any that keep to these rules, and one draw needn't show every extreme that they name: `field`: entries are finite real values.
All inputs are finite; a program needn't handle non-finite values.
Results may differ from a plain program's by a relative error of at most 0.00016.
Values sent between devices are 32-bit elements; how exact they have to be, the bound alone decides.
No kernel may reach another device: no remote copies, remote signals or barrier semaphores. Data moves between devices by JAX's collectives and lax.ppermute only.
A program may use at most 64 MiB of HBM per device.

v0:
```python
import jax
import jax.numpy as jnp
from jax import lax
from jax.sharding import PartitionSpec as P

ITERS = 2


def subspace(gram, start):
    block = start
    for turn in range(ITERS):
        image = jnp.dot(
            gram, block, precision=lax.Precision.HIGHEST, preferred_element_type=jnp.float32
        )
        small = jnp.dot(
            image.T, image, precision=lax.Precision.HIGHEST, preferred_element_type=jnp.float32
        )
        factor = jnp.linalg.cholesky(small)
        block = lax.linalg.triangular_solve(
            factor, image, left_side=False, lower=True, transpose_a=True
        )
    return block


def shards(field, start):
    regrouped = lax.all_to_all(field, "fibre", split_axis=1, concat_axis=0, tiled=True)
    rows_all = regrouped.shape[0]
    unfolded = regrouped.reshape(rows_all, -1)
    local_gram = jnp.dot(
        unfolded, unfolded.T, precision=lax.Precision.HIGHEST, preferred_element_type=jnp.float32
    )
    gram = lax.psum(local_gram, ("fibre", "col"))
    basis = subspace(gram, start)
    core = jnp.dot(
        basis.T, unfolded, precision=lax.Precision.HIGHEST, preferred_element_type=jnp.float32
    )
    return (basis, core.reshape(basis.shape[1], regrouped.shape[1], regrouped.shape[2]))


def solution(mesh):
    in_specs = (P("fibre", None, "col"), P())
    out_specs = (P(), P(None, "fibre", "col"))
    return jax.shard_map(shards, mesh=mesh, in_specs=in_specs, out_specs=out_specs, check_vma=False)
```

profile of v0, /device:TPU:24, one launch (start us, length us, event | category | flops | bytes accessed | tf_op | source)
XLA Modules:
  0.0 505.7 jit_solution(5928552759673224963)
XLA Ops:
  7.2 3.9 copy.7
  11.1 82.4 %all_to_all.15 = f32[40,160,128]{2,0,1:T(8,128)S(1)} all-to-all(f32[40,160,128]{2,0,1:T(8,128)S(1)} %copy.7), channel_id=1, replica_groups=mesh['fibre'=16,'col'=32] {'fibre'}, dimensions={1} | all-to-all | bytes 6553600 | tf_op jit(solution)/shard_map/all_to_all | solution.py:26
  93.5 0.8 copy.8
  94.3 2.3 copy-done.1
  96.6 10.5 %fusion = f32[640,640]{1,0:T(8,128)} fusion(f32[80,8,10,128]{3,2,1,0:T(8,128)S(1)} %bitcast.77), kind=kOutput, calls=%fused_computation.1 | convolution fusion | flops 6291456000 | bytes 4915200 | tf_op jit(solution)/shard_map/dot_general | solution.py:29
  107.2 5.8 %copy.18 = f32[80,8,10,128]{3,1,2,0:T(8,128)} copy(f32[80,8,10,128]{3,2,1,0:T(8,128)} %bitcast.78) | data formatting | bytes 6553600
  112.9 4.7 copy.11
  117.7 270.5 %all-reduce.5.cloned.1.call-done = f32[640,640]{1,0:T(8,128)} async-done(((f32[640,640]{1,0:T(8,128)}), f32[640,640]{1,0:T(8,128)}) %all-reduce.5.cloned.1.call-update) | async-done | bytes 1638416 | tf_op jit(solution)/shard_map/psum | solution.py:32
  388.1 3.3 fusion.30
  391.5 0.6 fusion.31
  392.2 11.7 %cholesky.136 = f32[128,128]{1,0:T(8,128)S(1)} custom-call(f32[128,128]{1,0:T(8,128)S(1)} %cholesky.208), custom_call_target="Cholesky" | custom-call | tf_op jit(solution)/shard_map/jit(cholesky)/cholesky | solution.py:18
  404.0 9.8 %custom-call.13 = f32[1,128,128]{1,2,0:T(8,128)S(1)} custom-call(f32[1,128,128]{2,1,0:T(8,128)S(1)} %get-tuple-element.33), custom_call_target="InvertDiagBlocksLowerTriangular" | custom-call | tf_op jit(solution)/shard_map/jit(cholesky)/cholesky | solution.py:18
  414.1 2.9 cholesky.156
  417.1 0.6 compare_reduce_fusion.2
  417.7 0.6 compare_reduce_fusion.3
  419.8 19.9 %custom-call.14 = f32[2,128,128]{1,2,0:T(8,128)S(1)} custom-call(f32[2,128,128]{2,1,0:T(8,128)S(1)} %pad_maximum_fusion.1), custom_call_target="InvertDiagBlocksLowerTriangular" | custom-call | tf_op jit(solution)/shard_map/triangular_solve/custom-call.0 | solution.py:19
  440.8 1.8 fusion.3
  443.3 11.7 %cholesky.174 = f32[128,128]{1,0:T(8,128)S(1)} custom-call(f32[128,128]{1,0:T(8,128)S(1)} %cholesky.211), custom_call_target="Cholesky" | custom-call | tf_op jit(solution)/shard_map/jit(cholesky)/cholesky | solution.py:18
  455.1 9.8 %custom-call.15 = f32[1,128,128]{1,2,0:T(8,128)S(1)} custom-call(f32[1,128,128]{2,1,0:T(8,128)S(1)} %get-tuple-element.31), custom_call_target="InvertDiagBlocksLowerTriangular" | custom-call | tf_op jit(solution)/shard_map/jit(cholesky)/cholesky | solution.py:18
  465.2 2.9 cholesky.194
  468.2 0.6 compare_reduce_fusion
  468.8 0.6 compare_reduce_fusion.1
  470.9 19.9 %custom-call.16 = f32[2,128,128]{1,2,0:T(8,128)S(1)} custom-call(f32[2,128,128]{2,1,0:T(8,128)S(1)} %pad_maximum_fusion.2), custom_call_target="InvertDiagBlocksLowerTriangular" | custom-call | tf_op jit(solution)/shard_map/triangular_solve/custom-call.0 | solution.py:19
  492.0 6.6 %fusion.7 = f32[160,10,128]{2,0,1:T(8,128)} fusion(f32[10,128,640]{2,1,0:T(8,128)} %bitcast.79, f32[640,160]{0,1:T(8,128)S(1)} %pad_maximum_fusion), kind=kOutput, calls=%fused_computation.13 | convolution fusion | flops 1572864000 | bytes 4505600 | tf_op jit(solution)/shard_map/dot_general | solution.py:34
  (44 shorter events, 4.1 us)
Async XLA Ops:
  7.2 381.0 %copy-start = (f32[640,160]{0,1:T(8,128)S(1)}, f32[640,160]{0,1:T(8,128)}, u32[]{:S(2)}) copy-start(f32[640,160]{0,1:T(8,128)} %param.6) | copy-start | bytes 1228804
  7.2 381.0 %all-reduce.5.cloned.1.call-start = ((), (), s32[]{:S(2)}) async-start(), calls=%async_computation.1 | async-start | bytes 3276800 | tf_op jit(solution)/shard_map/psum | solution.py:32
  94.2 2.3 copy-start.1
  388.1 52.6 %copy-start.2 = (f32[640,640]{1,0:T(8,128)S(1)}, f32[640,640]{1,0:T(8,128)}, u32[]{:S(2)}) copy-start(f32[640,640]{1,0:T(8,128)} %all-reduce.5.cloned.1.call-done) | copy-start | bytes 4915204
  491.9 6.6 %copy-start.3 = (f32[640,160]{0,1:T(8,128)}, f32[640,160]{0,1:T(8,128)S(1)}, u32[]{:S(2)}) copy-start(f32[640,160]{0,1:T(8,128)S(1)} %pad_maximum_fusion) | copy-start | bytes 1228804
Sparse Core Ops, SparseCore 0:
  107.3 280.8 all-reduce.4
where the time goes:
time: 508 us; the launch traced here: 506 us
  waiting for transfers between devices  270 us (53%)
  other arithmetic  91.7 us (18%)
  blocking collectives  82.4 us (16%)
  matrix products  26.1 us (5%)
  local copies, waits for them, and re-layouts  17.7 us (3%)
  between operations  17.2 us (3%)
    psum x1, waiting for transfers between devices, shards(): gram = lax.psum(local_gram, ('fibre', 'col'))  270 us
    all_to_all x1, blocking collectives, shards(): lax.all_to_all(field, 'fibre', split_axis=1, concat_axis=0, tiled=True)  82.4 us
    another operation x14, other arithmetic, subspace(): factor = jnp.linalg.cholesky(small)  51.6 us
    another operation x11, other arithmetic, subspace(): lax.linalg.triangular_solve(factor, image, left_side=False, lower=True, t...  40.1 us
    unnamed x10, local copies, waits for them, and re-layouts  12 us
    dot_general x1, matrix products, shards(): jnp.dot(unfolded, unfolded.T, precision=lax.Precision.HIGHEST, preferred_...  10.5 us
  transfers between devices with their start and end apart: 1, of which 1 were waited for; matrix products, arithmetic and copies ran while one was open for 2% of the time, Pallas kernels for 0%

commit v1 on v0

--- a/solution.py
+++ b/solution.py
@@ -23,7 +23,10 @@
 
 
 def shards(field, start):
-    regrouped = lax.all_to_all(field, "fibre", split_axis=1, concat_axis=0, tiled=True)
+    regrouped = jnp.concatenate(
+        lax.all_to_all(jnp.stack(jnp.split(field, lax.axis_size("fibre"), axis=1)), "fibre", 0, 0),
+        axis=0,
+    )
     rows_all = regrouped.shape[0]
     unfolded = regrouped.reshape(rows_all, -1)
     local_gram = jnp.dot(

time: 508 us -> 516 us (1.016); the launches traced: 506 us -> 506 us
    unnamed x10 -> x24, local copies, waits for them, and re-layouts: 12 us -> 9.05 us
where the time goes in v1:
time: 516 us; the launch traced here: 506 us
  waiting for transfers between devices  271 us (53%)
  other arithmetic  91.7 us (18%)
  blocking collectives  81.8 us (16%)
  matrix products  26.1 us (5%)
  local copies, waits for them, and re-layouts  18.5 us (4%)
  between operations  17.5 us (3%)
    psum x1, waiting for transfers between devices, shards(): gram = lax.psum(local_gram, ('fibre', 'col'))  271 us
    all_to_all x1, blocking collectives, shards(): lax.all_to_all(jnp.stack(jnp.split(field, lax.axis_size('fibre'), axis=1)...  81.8 us
    another operation x14, other arithmetic, subspace(): factor = jnp.linalg.cholesky(small)  51.6 us
    another operation x11, other arithmetic, subspace(): lax.linalg.triangular_solve(factor, image, left_side=False, lower=True, t...  40.1 us
    dot_general x1, matrix products, shards(): jnp.dot(unfolded, unfolded.T, precision=lax.Precision.HIGHEST, preferred_...  10.5 us
  transfers between devices with their start and end apart: 1, of which 1 were waited for; matrix products, arithmetic and copies ran while one was open for 2% of the time, Pallas kernels for 0%

profile of v1, /device:TPU:24, one launch (start us, length us, event | category | flops | bytes accessed | tf_op | source)
XLA Modules:
  0.0 506.3 jit_solution(15572728181197678426)
XLA Ops:
  7.2 3.6 fusion.46
  12.0 81.8 %all_to_all.5 = f32[16,40,10,128]{3,1,2,0:T(8,128)S(1)} all-to-all(f32[16,40,10,128]{3,1,2,0:T(8,128)S(1)} %fusion.13), channel_id=1, replica_groups=mesh['fibre'=16,'col'=32] {'fibre'}, dimensions={0} | all-to-all | bytes 6553600 | tf_op jit(solution)/shard_map/all_to_all | solution.py:27
  93.8 0.8 copy.26
  94.6 2.3 copy-done.1
  96.9 10.5 %fusion = f32[640,640]{1,0:T(8,128)} fusion(f32[80,8,10,128]{3,2,1,0:T(8,128)S(1)} %bitcast.138), kind=kOutput, calls=%fused_computation.1 | convolution fusion | flops 6291456000 | bytes 4915200 | tf_op jit(solution)/shard_map/dot_general | solution.py:32
  107.5 5.8 %copy.100 = f32[80,8,10,128]{3,1,2,0:T(8,128)} copy(f32[80,8,10,128]{3,2,1,0:T(8,128)} %bitcast.139) | data formatting | bytes 6553600
  113.3 4.7 copy.29
  118.0 270.6 %all-reduce.5.cloned.1.call-done = f32[640,640]{1,0:T(8,128)} async-done(((f32[640,640]{1,0:T(8,128)}), f32[640,640]{1,0:T(8,128)}) %all-reduce.5.cloned.1.call-update) | async-done | bytes 1638416 | tf_op jit(solution)/shard_map/psum | solution.py:35
  388.6 3.3 fusion.47
  391.9 0.6 fusion.48
  392.7 11.7 %cholesky.136 = f32[128,128]{1,0:T(8,128)S(1)} custom-call(f32[128,128]{1,0:T(8,128)S(1)} %cholesky.208), custom_call_target="Cholesky" | custom-call | tf_op jit(solution)/shard_map/jit(cholesky)/cholesky | solution.py:18
  404.4 9.8 %custom-call.13 = f32[1,128,128]{1,2,0:T(8,128)S(1)} custom-call(f32[1,128,128]{2,1,0:T(8,128)S(1)} %get-tuple-element.49), custom_call_target="InvertDiagBlocksLowerTriangular" | custom-call | tf_op jit(solution)/shard_map/jit(cholesky)/cholesky | solution.py:18
  414.6 2.9 cholesky.156
  417.5 0.6 compare_reduce_fusion.2
  418.2 0.6 compare_reduce_fusion.3
  420.3 19.9 %custom-call.14 = f32[2,128,128]{1,2,0:T(8,128)S(1)} custom-call(f32[2,128,128]{2,1,0:T(8,128)S(1)} %pad_maximum_fusion.1), custom_call_target="InvertDiagBlocksLowerTriangular" | custom-call | tf_op jit(solution)/shard_map/triangular_solve/custom-call.0 | solution.py:19
  441.2 1.8 fusion.3
  443.8 11.7 %cholesky.174 = f32[128,128]{1,0:T(8,128)S(1)} custom-call(f32[128,128]{1,0:T(8,128)S(1)} %cholesky.211), custom_call_target="Cholesky" | custom-call | tf_op jit(solution)/shard_map/jit(cholesky)/cholesky | solution.py:18
  455.5 9.8 %custom-call.15 = f32[1,128,128]{1,2,0:T(8,128)S(1)} custom-call(f32[1,128,128]{2,1,0:T(8,128)S(1)} %get-tuple-element.47), custom_call_target="InvertDiagBlocksLowerTriangular" | custom-call | tf_op jit(solution)/shard_map/jit(cholesky)/cholesky | solution.py:18
  465.7 2.9 cholesky.194
  468.6 0.6 compare_reduce_fusion
  469.3 0.6 compare_reduce_fusion.1
  471.4 19.9 %custom-call.16 = f32[2,128,128]{1,2,0:T(8,128)S(1)} custom-call(f32[2,128,128]{2,1,0:T(8,128)S(1)} %pad_maximum_fusion.2), custom_call_target="InvertDiagBlocksLowerTriangular" | custom-call | tf_op jit(solution)/shard_map/triangular_solve/custom-call.0 | solution.py:19
  492.4 6.6 %fusion.7 = f32[160,10,128]{2,0,1:T(8,128)} fusion(f32[10,128,640]{2,1,0:T(8,128)} %bitcast.140, f32[640,160]{0,1:T(8,128)S(1)} %pad_maximum_fusion), kind=kOutput, calls=%fused_computation.13 | convolution fusion | flops 1572864000 | bytes 4505600 | tf_op jit(solution)/shard_map/dot_general | solution.py:37
  (60 shorter events, 5.1 us)
Async XLA Ops:
  7.2 381.4 %copy-start = (f32[640,160]{0,1:T(8,128)S(1)}, f32[640,160]{0,1:T(8,128)}, u32[]{:S(2)}) copy-start(f32[640,160]{0,1:T(8,128)} %param.6) | copy-start | bytes 1228804
  7.2 381.4 %all-reduce.5.cloned.1.call-start = ((), (), s32[]{:S(2)}) async-start(), calls=%async_computation.1 | async-start | bytes 3276800 | tf_op jit(solution)/shard_map/psum | solution.py:35
  94.6 2.3 copy-start.1
  388.6 52.6 %copy-start.2 = (f32[640,640]{1,0:T(8,128)S(1)}, f32[640,640]{1,0:T(8,128)}, u32[]{:S(2)}) copy-start(f32[640,640]{1,0:T(8,128)} %all-reduce.5.cloned.1.call-done) | copy-start | bytes 4915204
  492.4 6.6 %copy-start.3 = (f32[640,160]{0,1:T(8,128)}, f32[640,160]{0,1:T(8,128)S(1)}, u32[]{:S(2)}) copy-start(f32[640,160]{0,1:T(8,128)S(1)} %pad_maximum_fusion) | copy-start | bytes 1228804
Sparse Core Ops, SparseCore 0:
  107.6 280.9 all-reduce.4
